TPU v7x, 256 devices: a whole 4x4x8 slice. The times are simulated.
256 devices in a mesh: gx: 8 (over z), gy: 16 (over y, x), sa: 2 (over core).
Axes of the slice: x: 4, y: 4, z: 8, core: 2. Of those that a mesh axis runs over, the one named last changes fastest.
Arguments:
- field: float32 [33, 32, 672, 256], P(None, 'gx', 'gy', 'sa'), as said below
- start: float32 [33, 16], replicated, may hold values from -1 to 1
Outputs:
- basis: float32 [33, 16], replicated
- gram_two: float32 [672, 672], P('gy', ('gx', 'sa'))
Inputs may be any that keep to these rules, and one draw needn't show every extreme that they name: `field`: every entry is finite; species differ in scale.
All inputs are finite; a program needn't handle non-finite values.
Results may differ from a plain program's by a relative error of at most 0.0003.
Values sent between devices are 32-bit elements; how exact they have to be, the bound alone decides.
A program may use at most 128 MiB of HBM per device.

v0:
```python
import jax
import jax.numpy as jnp
from jax import lax
from jax.sharding import PartitionSpec as P

ITERS = 4
HIGH = lax.Precision.HIGHEST


def orth(block):
    inner = jnp.dot(block.T, block, precision=HIGH, preferred_element_type=jnp.float32)
    lower = jnp.linalg.cholesky(inner)
    return jax.scipy.linalg.solve_triangular(lower, block.T, lower=True).T


def leading(gram, start, rounds):
    basis = orth(orth(start))
    for step in range(rounds):
        basis = orth(orth(jnp.dot(gram, basis, precision=HIGH, preferred_element_type=jnp.float32)))
    return basis


def project(basis, data):
    return jnp.einsum("sr,sxyz->rxyz", basis, data, precision=HIGH)


def line_gram(left, right):
    return jnp.einsum("rxiz,rxjz->ij", left, right, precision=HIGH)


def on_device(field, start):
    species, cells_x, cells_y, cells_z = field.shape
    ranks = start.shape[1]
    total_x = cells_x * lax.axis_size("gx")
    total_y = cells_y * lax.axis_size("gy")
    total_z = cells_z * lax.axis_size("sa")
    flat = field.reshape(species, -1)
    partial_gram = jnp.dot(flat, flat.T, precision=HIGH, preferred_element_type=jnp.float32)
    species_gram = lax.psum(partial_gram, ("gx", "gy", "sa")) / (total_x * total_y * total_z)
    basis = leading(species_gram, start, ITERS)
    core = project(basis, field)
    part_block = line_gram(core, lax.all_gather(core, "gy", axis=2, tiled=True))
    block = lax.psum_scatter(part_block, ("gx", "sa"), scatter_dimension=1, tiled=True) / (
        ranks * total_x * total_z
    )
    return (basis, block)


def solution(mesh):
    in_specs = (P(None, "gx", "gy", "sa"), P())
    out_specs = (P(), P("gy", ("gx", "sa")))
    return jax.shard_map(
        on_device, mesh=mesh, in_specs=in_specs, out_specs=out_specs, check_vma=False
    )
```

profile of v0, /device:TPU:1, one launch (start us, length us, event | category | flops | bytes accessed | tf_op | source)
XLA Modules:
  0.0 422.5 jit_solution(17980562996375337005)
XLA Ops:
  7.2 0.6 copy-done
  8.1 1.5 cholesky.164
  9.6 0.6 compare_reduce_fusion.9
  10.2 0.6 fusion.27
  10.9 1.2 custom-call.14
  12.1 0.2 fusion.69
  12.5 1.5 cholesky.175
  14.0 0.6 compare_reduce_fusion.8
  14.7 0.6 fusion.28
  15.3 1.2 custom-call.15
  16.6 0.2 fusion.66
  16.8 6.2 %fusion.12 = f32[33,33]{1,0:T(8,128)S(1)} fusion(f32[33,4,42,128]{3,1,2,0:T(4,128)} %param.5), kind=kOutput, calls=%fused_computation.8 | convolution fusion | flops 281014272 | bytes 2842884 | tf_op jit(solution)/shard_map/dot_general | solution.py:38
  22.9 81.5 %psum.7 = f32[33,33]{1,0:T(8,128)S(1)} all-reduce(f32[33,33]{1,0:T(8,128)S(1)} %fusion.12), channel_id=1, replica_groups=mesh['gx'=8,'gy'=16,'sa'=2] {'gx','gy','sa'}, use_global_device_ids=true, to_apply=%region_0.0 | all-reduce | flops 1089 | bytes 8712 | tf_op jit(solution)/shard_map/psum | solution.py:39
  104.6 0.1 fusion.97
  104.8 1.5 cholesky.186
  106.3 0.6 compare_reduce_fusion.7
  107.0 0.6 fusion.29
  107.6 1.2 custom-call.16
  108.9 0.2 fusion.62
  109.3 1.5 cholesky.197
  110.8 0.6 compare_reduce_fusion.6
  111.4 0.6 fusion.30
  112.1 1.2 custom-call.17
  113.3 0.2 fusion.59
  113.5 0.2 fusion.19
  113.9 1.5 cholesky.208
  115.4 0.6 compare_reduce_fusion.5
  116.0 0.6 fusion.31
  116.7 1.2 custom-call.18
  117.9 0.2 fusion.55
  118.4 1.5 cholesky.219
  119.9 0.6 compare_reduce_fusion.4
  120.5 0.6 fusion.32
  121.2 1.2 custom-call.19
  122.4 0.2 fusion.52
  122.6 0.2 fusion.17
  123.0 1.5 cholesky.230
  124.5 0.6 compare_reduce_fusion.3
  125.1 0.6 fusion.33
  125.8 1.2 custom-call.20
  127.0 0.2 fusion.48
  127.4 1.5 cholesky.241
  128.9 0.6 compare_reduce_fusion.2
  129.6 0.6 fusion.34
  130.2 1.2 custom-call.21
  131.5 0.2 fusion.45
  131.7 0.2 fusion.15
  132.0 1.5 cholesky.252
  133.5 0.6 compare_reduce_fusion.1
  134.2 0.6 fusion.35
  134.9 1.2 custom-call.22
  136.1 0.2 fusion.41
  136.5 1.5 cholesky.263
  138.0 0.6 compare_reduce_fusion
  138.7 0.6 fusion.36
  139.3 1.2 custom-call.23
  140.5 0.2 fusion.38
  140.8 3.4 fusion.2
  144.2 0.2 all-reduce.3.cloned.1.call-start
  144.4 138.0 %all-gather.2.cloned.1.call-done = f32[16,4,672,128]{3,0,2,1:T(8,128)} async-done(((f32[16,4,42,128]{3,0,2,1:T(8,128)}), f32[16,4,672,128]{3,0,2,1:T(8,128)}) %all-gather.2.cloned.1.call-update) | async-done | bytes 22020112 | tf_op jit(solution)/shard_map/all_gather | solution.py:42
  282.4 29.2 %fusion.7 = f32[42,672]{1,0:T(8,128)} fusion(f32[16,4,672,128]{3,0,2,1:T(8,128)} %all-gather.2.cloned.1.call-done, f32[16,4,42,128]{3,0,2,1:T(8,128)} %fusion.2), kind=kOutput, calls=%fused_computation.7 | convolution fusion | flops 2774532096 | bytes 23509248 | tf_op jit(solution)/shard_map/rxiz,rxjz->ij/dot_general | solution.py:28
  311.6 0.6 dynamic-slice
  312.9 101.3 %all-reduce.3.cloned.1.call-done = f32[42,672]{1,0:T(8,128)} async-done(((f32[42,672]{1,0:T(8,128)}), f32[42,672]{1,0:T(8,128)}) %all-reduce.3.cloned.1.call-update) | async-done | bytes 112912
  414.2 1.5 dynamic-slice_multiply_fusion
  (50 shorter events, 2.6 us)
Async XLA Ops:
  7.2 0.7 copy-start
  7.2 133.6 %copy-start.1 = (f32[33,4,42,128]{3,1,2,0:T(4,128)S(1)}, f32[33,4,42,128]{3,1,2,0:T(4,128)}, u32[]{:S(2)}) copy-start(f32[33,4,42,128]{3,1,2,0:T(4,128)} %param.5) | copy-start | bytes 8515588
  7.2 275.2 %all-gather.2.cloned.1.call-start = ((), (), s32[]{:S(2)}) async-start(), calls=%async_computation | async-start | bytes 23396352 | tf_op jit(solution)/shard_map/all_gather | solution.py:42
  140.7 3.4 copy-start.2
  144.2 167.4 %copy-start.3 = (u32[256]{0:T(256)S(1)}, u32[256]{0:T(256)}, u32[]{:S(2)}) copy-start(u32[256]{0:T(256)} %constant.40) | copy-start | bytes 3076
  144.2 270.0 %all-reduce.3.cloned.1.call-start = ((), (), s32[]{:S(2)}) async-start(), calls=%async_computation.1 | async-start | bytes 294912
Sparse Core Ops, SparseCore 0:
  144.3 138.0 all-gather.1
  311.7 102.3 all-reduce.2
where the time goes:
time: 423 us; the launch traced here: 422 us
  waiting for transfers between devices  239 us (57%)
  blocking collectives  81.5 us (19%)
  matrix products  42.7 us (10%)
  other arithmetic  41.8 us (10%)
  between operations  14.9 us (4%)
    all_gather x1, waiting for transfers between devices, on_device(): part_block = line_gram(core, lax.all_gather(core, 'gy', axis=2, tiled=True))  138 us
    unnamed x3, waiting for transfers between devices  101 us
    psum x1, blocking collectives, on_device(): lax.psum(partial_gram, ('gx', 'gy', 'sa')) / (total_x * total_y * total_z)  81.5 us
    dot_general x1, matrix products, line_gram(): return jnp.einsum('rxiz,rxjz->ij', left, right, precision=HIGH)  29.2 us
    another operation x30, other arithmetic, orth(): lower = jnp.linalg.cholesky(inner)  21.5 us
    another operation x20, other arithmetic, orth(): return jax.scipy.linalg.solve_triangular(lower, block.T, lower=True).T  18.8 us
  transfers between devices with their start and end apart: 2, of which 2 were waited for; matrix products, arithmetic and copies ran while one was open for 0% of the time, Pallas kernels for 0%

commit v1 on v0

--- a/solution.py
+++ b/solution.py
@@ -36,7 +36,9 @@
     total_z = cells_z * lax.axis_size("sa")
     flat = field.reshape(species, -1)
     partial_gram = jnp.dot(flat, flat.T, precision=HIGH, preferred_element_type=jnp.float32)
-    species_gram = lax.psum(partial_gram, ("gx", "gy", "sa")) / (total_x * total_y * total_z)
+    species_gram = lax.psum(lax.psum(partial_gram, ("gy", "sa")), "gx") / (
+        total_x * total_y * total_z
+    )
     basis = leading(species_gram, start, ITERS)
     core = project(basis, field)
     part_block = line_gram(core, lax.all_gather(core, "gy", axis=2, tiled=True))

time: 423 us -> 501 us (1.18)
  blocking collectives: 81.5 us -> 150 us
  waiting for transfers between devices: 239 us -> 249 us
    psum x1 -> x2, blocking collectives: 81.5 us -> 150 us  [the longest x1 124 us: on_device(): lax.psum(partial_gram, ('gy', 'sa'))]
    all_gather x1, waiting for transfers between devices: 138 us -> 147 us  [on_device(): part_block = line_gram(core, lax.all_gather(core, 'gy', axis=2, tiled=True))]
where the time goes in v1:
time: 501 us
  waiting for transfers between devices  249 us (50%)
  blocking collectives  150 us (30%)
  matrix products  42.7 us (9%)
  other arithmetic  41.8 us (8%)
  between operations  14.9 us (3%)
    all_gather x1, waiting for transfers between devices, on_device(): part_block = line_gram(core, lax.all_gather(core, 'gy', axis=2, tiled=True))  147 us
    psum x1, blocking collectives, on_device(): lax.psum(partial_gram, ('gy', 'sa'))  124 us
    unnamed x3, waiting for transfers between devices  101 us
    dot_general x1, matrix products, line_gram(): return jnp.einsum('rxiz,rxjz->ij', left, right, precision=HIGH)  29.2 us
    psum x1, blocking collectives, on_device(): lax.psum(lax.psum(partial_gram, ('gy', 'sa')), 'gx')  26 us
    another operation x30, other arithmetic, orth(): lower = jnp.linalg.cholesky(inner)  21.5 us
    another operation x20, other arithmetic, orth(): return jax.scipy.linalg.solve_triangular(lower, block.T, lower=True).T  18.8 us
  transfers between devices with their start and end apart: 2, of which 2 were waited for; matrix products, arithmetic and copies ran while one was open for 0% of the time, Pallas kernels for 0%

profile of v1, /device:TPU:1, one launch (start us, length us, event | category | flops | bytes accessed | tf_op | source)
XLA Modules:
  0.0 500.7 jit_solution(18278713739232230433)
XLA Ops:
  7.2 0.6 copy-done
  8.1 1.5 cholesky.164
  9.6 0.6 compare_reduce_fusion.9
  10.2 0.6 fusion.27
  10.9 1.2 custom-call.14
  12.1 0.2 fusion.69
  12.5 1.5 cholesky.175
  14.0 0.6 compare_reduce_fusion.8
  14.7 0.6 fusion.28
  15.3 1.2 custom-call.15
  16.6 0.2 fusion.66
  16.8 6.2 %fusion.12 = f32[33,33]{1,0:T(8,128)S(1)} fusion(f32[33,4,42,128]{3,1,2,0:T(4,128)} %param.5), kind=kOutput, calls=%fused_computation.8 | convolution fusion | flops 281014272 | bytes 2842884 | tf_op jit(solution)/shard_map/dot_general | solution.py:38
  22.9 124.2 %psum.14 = f32[33,33]{1,0:T(8,128)S(1)} all-reduce(f32[33,33]{1,0:T(8,128)S(1)} %fusion.12), channel_id=1, replica_groups=mesh['gx'=8,'gy'=16,'sa'=2] {'gy','sa'}, use_global_device_ids=true, to_apply=%region_0.0 | all-reduce | flops 1089 | bytes 8712 | tf_op jit(solution)/shard_map/psum | solution.py:39
  147.2 26.0 %psum.15 = f32[33,33]{1,0:T(8,128)S(1)} all-reduce(f32[33,33]{1,0:T(8,128)S(1)} %psum.14), channel_id=1, replica_groups=mesh['gx'=8,'gy'=16,'sa'=2] {'gx'}, use_global_device_ids=true, to_apply=%region_1.0 | all-reduce | flops 1089 | bytes 8712 | tf_op jit(solution)/shard_map/psum | solution.py:39
  173.6 1.5 cholesky.186
  175.1 0.6 compare_reduce_fusion.7
  175.7 0.6 fusion.29
  176.4 1.2 custom-call.16
  177.6 0.2 fusion.62
  178.0 1.5 cholesky.197
  179.5 0.6 compare_reduce_fusion.6
  180.2 0.6 fusion.30
  180.8 1.2 custom-call.17
  182.1 0.2 fusion.59
  182.3 0.2 fusion.19
  182.6 1.5 cholesky.208
  184.2 0.6 compare_reduce_fusion.5
  184.8 0.6 fusion.31
  185.5 1.2 custom-call.18
  186.7 0.2 fusion.55
  187.1 1.5 cholesky.219
  188.6 0.6 compare_reduce_fusion.4
  189.3 0.6 fusion.32
  189.9 1.2 custom-call.19
  191.1 0.2 fusion.52
  191.3 0.2 fusion.17
  191.7 1.5 cholesky.230
  193.2 0.6 compare_reduce_fusion.3
  193.9 0.6 fusion.33
  194.5 1.2 custom-call.20
  195.8 0.2 fusion.48
  196.2 1.5 cholesky.241
  197.7 0.6 compare_reduce_fusion.2
  198.3 0.6 fusion.34
  199.0 1.2 custom-call.21
  200.2 0.2 fusion.45
  200.4 0.2 fusion.15
  200.8 1.5 cholesky.252
  202.3 0.6 compare_reduce_fusion.1
  202.9 0.6 fusion.35
  203.6 1.2 custom-call.22
  204.8 0.2 fusion.41
  205.3 1.5 cholesky.263
  206.8 0.6 compare_reduce_fusion
  207.4 0.6 fusion.36
  208.1 1.2 custom-call.23
  209.3 0.2 fusion.38
  209.5 3.4 fusion.2
  212.9 0.2 all-reduce.3.cloned.1.call-start
  213.2 147.5 %all-gather.2.cloned.1.call-done = f32[16,4,672,128]{3,0,2,1:T(8,128)} async-done(((f32[16,4,42,128]{3,0,2,1:T(8,128)}), f32[16,4,672,128]{3,0,2,1:T(8,128)}) %all-gather.2.cloned.1.call-update) | async-done | bytes 22020112 | tf_op jit(solution)/shard_map/all_gather | solution.py:44
  360.6 29.2 %fusion.7 = f32[42,672]{1,0:T(8,128)} fusion(f32[16,4,672,128]{3,0,2,1:T(8,128)} %all-gather.2.cloned.1.call-done, f32[16,4,42,128]{3,0,2,1:T(8,128)} %fusion.2), kind=kOutput, calls=%fused_computation.7 | convolution fusion | flops 2774532096 | bytes 23509248 | tf_op jit(solution)/shard_map/rxiz,rxjz->ij/dot_general | solution.py:28
  389.9 0.6 dynamic-slice
  391.1 101.3 %all-reduce.3.cloned.1.call-done = f32[42,672]{1,0:T(8,128)} async-done(((f32[42,672]{1,0:T(8,128)}), f32[42,672]{1,0:T(8,128)}) %all-reduce.3.cloned.1.call-update) | async-done | bytes 112912
  492.4 1.5 dynamic-slice_multiply_fusion
  (51 shorter events, 2.7 us)
Async XLA Ops:
  7.2 0.7 copy-start
  7.2 202.3 %copy-start.1 = (f32[33,4,42,128]{3,1,2,0:T(4,128)S(1)}, f32[33,4,42,128]{3,1,2,0:T(4,128)}, u32[]{:S(2)}) copy-start(f32[33,4,42,128]{3,1,2,0:T(4,128)} %param.5) | copy-start | bytes 8515588
  7.2 353.5 %all-gather.2.cloned.1.call-start = ((), (), s32[]{:S(2)}) async-start(), calls=%async_computation | async-start | bytes 23396352 | tf_op jit(solution)/shard_map/all_gather | solution.py:44
  209.5 3.4 copy-start.2
  212.9 176.9 %copy-start.3 = (u32[256]{0:T(256)S(1)}, u32[256]{0:T(256)}, u32[]{:S(2)}) copy-start(u32[256]{0:T(256)} %constant.40) | copy-start | bytes 3076
  212.9 279.5 %all-reduce.3.cloned.1.call-start = ((), (), s32[]{:S(2)}) async-start(), calls=%async_computation.1 | async-start | bytes 294912
Sparse Core Ops, SparseCore 0:
  213.0 147.5 all-gather.1
  390.0 102.3 all-reduce.2
